TPU v7x, 512 devices: a whole 4x8x8 slice. The times are simulated.
512 devices in a mesh: row: 128 (over z, y, core), ex: 4 (over x).
Axes of the slice: x: 4, y: 8, z: 8, core: 2. Of those that a mesh axis runs over, the one named last changes fastest.
Arguments:
- grads: bfloat16 [1, 4, 2048, 2048], P(None, 'ex', 'row'), may hold values from -6 to 6
- right_inv: bfloat16 [2048, 2048], P('row', 'ex'), may hold values from -0.125 to 0.125
- left_inv: bfloat16 [2048, 2048], P(('row', 'ex')), may hold values from -0.125 to 0.125
- row_signs: int32 [1, 4, 2048], replicated, may hold values from 0 to 1
- col_signs: int32 [1, 4, 2048], replicated, may hold values from 0 to 1
- listed: int32 [1, 128, 4, 32], P(None, 'row', 'ex'), may hold values from 0 to 32767, as said below
- owners: int32 [1, 128, 4, 32, 1], P(None, 'row'), may hold values from 0 to 127; in each aligned block of 128 rows (0 to 127, 128 to 255, ..., all dimensions but the last counted through in order) at most 2 rows name the same one
Outputs:
- sketch: float32 [1, 128, 128, 2, 256], P(None, 'row')
Inputs may be any that keep to these rules, and one draw needn't show every extreme that they name: `listed`: for each batch b, group g and example x, the 32 entries name distinct blocks in ascending order, all from g * 256 to (g + 1) * 256 - 1. `owners`: within one batch and group, no owner is named by more than 2 of the 128 entries, a bound that some block reaches.
All inputs are finite; a program needn't handle non-finite values.
Results may differ from a plain program's by a relative error of at most 0.0029.
Values may be sent and summed in bfloat16 or wider, within the bound.
No kernel may reach another device: no remote copies, remote signals or barrier semaphores. Data moves between devices by JAX's collectives and lax.ppermute only.
A program may use at most 64 MiB of HBM per device.

v0:
```python
import math
import jax
import jax.numpy as jnp
from jax import lax
from jax.sharding import PartitionSpec as P

FA = 32
FB = 64
BLOCK = 128
highest = lax.Precision.HIGHEST


def dft_tables(length):
    counter = jnp.arange(length, dtype=jnp.int32)
    phase_index = counter[:, None] * counter[None, :] % length
    angles = phase_index.astype(jnp.float32) * (2.0 * math.pi / length)
    return (jnp.cos(angles), -jnp.sin(angles))


def twiddle_table(first_len, second_len, total):
    phase_index = (
        jnp.arange(first_len, dtype=jnp.int32)[:, None]
        * jnp.arange(second_len, dtype=jnp.int32)[None, :]
    )
    angles = phase_index.astype(jnp.float32) * (2.0 * math.pi / total)
    return (jnp.cos(angles), -jnp.sin(angles))


def complex_mul(real_a, imag_a, real_b, imag_b):
    return (real_a * real_b - imag_a * imag_b, real_a * imag_b + imag_a * real_b)


def column_transform(flipped, tables):
    first_cos, first_sin, mid_cos, mid_sin, last_cos, last_sin = tables
    lanes = flipped.shape[0]
    spatial = flipped.reshape(lanes, FA, FB)
    real_one = jnp.einsum("pk,jpq->jkq", first_cos, spatial, precision=highest)
    imag_one = jnp.einsum("pk,jpq->jkq", first_sin, spatial, precision=highest)
    real_two, imag_two = complex_mul(real_one, imag_one, mid_cos[None], mid_sin[None])
    real_out = jnp.einsum("qm,jkq->jmk", last_cos, real_two, precision=highest) - jnp.einsum(
        "qm,jkq->jmk", last_sin, imag_two, precision=highest
    )
    imag_out = jnp.einsum("qm,jkq->jmk", last_sin, real_two, precision=highest) + jnp.einsum(
        "qm,jkq->jmk", last_cos, imag_two, precision=highest
    )
    return (real_out.reshape(lanes, FA * FB), imag_out.reshape(lanes, FA * FB))


def row_transform(real_in, imag_in, tables):
    first_cos, first_sin, mid_cos, mid_sin, last_cos, last_sin = tables
    lanes = real_in.shape[1]
    real_grid = real_in.reshape(FA, FB, lanes)
    imag_grid = imag_in.reshape(FA, FB, lanes)
    real_one = jnp.einsum("pk,pql->kql", first_cos, real_grid, precision=highest) - jnp.einsum(
        "pk,pql->kql", first_sin, imag_grid, precision=highest
    )
    imag_one = jnp.einsum("pk,pql->kql", first_sin, real_grid, precision=highest) + jnp.einsum(
        "pk,pql->kql", first_cos, imag_grid, precision=highest
    )
    real_two, imag_two = complex_mul(real_one, imag_one, mid_cos[:, :, None], mid_sin[:, :, None])
    real_out = jnp.einsum("qm,kql->lmk", last_cos, real_two, precision=highest) - jnp.einsum(
        "qm,kql->lmk", last_sin, imag_two, precision=highest
    )
    imag_out = jnp.einsum("qm,kql->lmk", last_sin, real_two, precision=highest) + jnp.einsum(
        "qm,kql->lmk", last_cos, imag_two, precision=highest
    )
    return (real_out.reshape(lanes, FA * FB), imag_out.reshape(lanes, FA * FB))


def shards(grads, right_inv, left_inv, row_signs, col_signs, listed, owners):
    row_count = lax.axis_size("row")
    ex_count = lax.axis_size("ex")
    row_id = lax.axis_index("row")
    ex_id = lax.axis_index("ex")
    local_rows = grads.shape[2]
    width = grads.shape[3]
    ex_cols = right_inv.shape[1]
    list_len = listed.shape[3]
    block_count = local_rows * (width // BLOCK)
    capacity = max(2, 2 * ex_count * list_len // row_count)
    right_cols = lax.all_gather(right_inv, "row", axis=0, tiled=True)
    left_full = lax.all_gather(left_inv, ("row", "ex"), axis=0, tiled=True)
    pair_start = row_id * local_rows
    my_example = pair_start // ex_cols
    col_start = ex_id * ex_cols + pair_start % ex_cols
    first_cos, first_sin = dft_tables(FA)
    mid_cos, mid_sin = twiddle_table(FA, FB, width)
    last_cos, last_sin = dft_tables(FB)
    tables = (first_cos, first_sin, mid_cos, mid_sin, last_cos, last_sin)
    columns = col_start + jnp.arange(local_rows, dtype=jnp.int32)
    cross_phase = columns[:, None] * jnp.arange(width, dtype=jnp.int32)[None, :]
    cross_angle = cross_phase.astype(jnp.float32) * (2.0 * math.pi / (width * width))
    cross_cos = jnp.cos(cross_angle)
    cross_sin = -jnp.sin(cross_angle)
    entry_order = jnp.arange(ex_count * list_len, dtype=jnp.int32)
    before = entry_order[:, None] < entry_order[None, :]
    own_rows = grads[0]
    rows_all = lax.all_gather(own_rows, "ex", axis=0, tiled=True)
    projected = jnp.einsum(
        "xrk,kc->xcr", rows_all, right_cols, preferred_element_type=jnp.float32
    ).astype(jnp.bfloat16)
    projected = projected.reshape(ex_count * ex_cols, local_rows)
    pair_cols = lax.all_to_all(projected, "row", split_axis=0, concat_axis=1, tiled=True)
    whitened = lax.dot_general(
        pair_cols, left_full, (((1,), (1,)), ((), ())), preferred_element_type=jnp.float32
    )
    row_bits = lax.dynamic_index_in_dim(row_signs[0], my_example, 0, keepdims=False)
    col_bits = lax.dynamic_slice(col_signs[0], (my_example, col_start), (1, local_rows))[0]
    row_flip = (1 - 2 * row_bits).astype(jnp.float32)
    col_flip = (1 - 2 * col_bits).astype(jnp.float32)
    flipped = whitened * row_flip[None, :] * col_flip[:, None]
    real_one, imag_one = column_transform(flipped, tables)
    real_two, imag_two = complex_mul(real_one, imag_one, cross_cos, cross_sin)
    stacked = jnp.stack([real_two, imag_two])
    arrived_rows = lax.all_to_all(
        lax.all_to_all(stacked, "row", split_axis=2, concat_axis=1, tiled=True),
        "ex",
        split_axis=1,
        concat_axis=1,
        tiled=True,
    )
    real_four, imag_four = row_transform(arrived_rows[0], arrived_rows[1], tables)
    real_four = real_four / width
    imag_four = imag_four / width
    packed = jnp.concatenate(
        [real_four.reshape(block_count, BLOCK), imag_four.reshape(block_count, BLOCK)], axis=1
    )
    local_ids = listed[0, 0, 0] - row_id * block_count
    picked = jnp.take(packed, local_ids, axis=0)
    entries = lax.all_gather(picked, "ex", axis=0, tiled=True)
    owner_ids = owners[0, 0, :, :, 0].reshape(-1)
    same = owner_ids[:, None] == owner_ids[None, :]
    slot_index = jnp.sum(same & before, axis=0)
    position = owner_ids * capacity + slot_index
    outgoing = jnp.zeros((row_count * capacity, 2 * BLOCK), jnp.float32).at[position].set(entries)
    arrived = lax.all_to_all(outgoing, "row", split_axis=0, concat_axis=0, tiled=True)
    stores = [arrived.reshape(1, row_count, capacity, 2 * BLOCK)]
    return jnp.stack(stores)


def solution(mesh):
    in_specs = (
        P(None, "ex", "row", None),
        P("row", "ex"),
        P(("row", "ex"), None),
        P(),
        P(),
        P(None, "row", "ex", None),
        P(None, "row", None, None, None),
    )
    out_specs = P(None, "row", None, None, None)
    return jax.shard_map(shards, mesh=mesh, in_specs=in_specs, out_specs=out_specs, check_vma=False)
```

profile of v0, /device:TPU:1, one launch (start us, length us, event | category | flops | bytes accessed | tf_op | source)
XLA Modules:
  0.0 361.3 jit_solution(6742715925657476330)
XLA Ops:
  6.5 0.7 all-gather.5.cloned.1.call-update
  7.3 0.7 all-gather.7.cloned.1.call-update
  8.0 10.7 %all-gather = bf16[4,1,16,2048]{3,2,1,0:T(8,128)(2,1)S(1)} all-gather(bf16[1,1,16,2048]{3,2,1,0:T(8,128)(2,1)} %param.7), channel_id=2, replica_groups=mesh['row'=128,'ex'=4] {'ex'}, dimensions={0}, use_global_device_ids=true | all-gather | bytes 327680 | tf_op jit(solution)/shard_map/all_gather | solution.py:98
  18.8 0.7 fusion.70
  19.5 0.8 subtract_convert_fusion
  20.2 79.2 %all-gather.5.cloned.1.call-done = bf16[2048,512]{1,0:T(8,128)(2,1)} async-done(((bf16[16,512]{1,0:T(8,128)(2,1)}), bf16[2048,512]{1,0:T(8,128)(2,1)}) %all-gather.5.cloned.1.call-update) | async-done | bytes 2097168 | tf_op jit(solution)/shard_map/all_gather | solution.py:81
  99.4 2.1 fusion.12
  102.3 1.0 reshape.326
  103.3 9.4 %all-to-all-start = ((bf16[128,2,128]{2,1,0:T(2,128)(2,1)}), bf16[128,2,128]{2,1,0:T(2,128)(2,1)S(1)}, u32[]{:S(2)}, u32[]{:S(2)}) async-start(bf16[128,2,128]{2,1,0:T(2,128)(2,1)} %reshape.326), calls=%async_computation | async-start | bytes 131072 | tf_op jit(solution)/shard_map/all_to_all | solution.py:103
  112.7 0.8 convert_bitcast_fusion
  113.6 10.6 %all-to-all-done = bf16[128,2,128]{2,1,0:T(2,128)(2,1)S(1)} async-done(((bf16[128,2,128]{2,1,0:T(2,128)(2,1)}), bf16[128,2,128]{2,1,0:T(2,128)(2,1)S(1)}, u32[]{:S(2)}, u32[]{:S(2)}) %all-to-all-start) | async-done | bytes 65568 | tf_op jit(solution)/shard_map/all_to_all | solution.py:103
  124.5 104.7 %all-gather.7.cloned.1.call-done = bf16[512,4,2048]{2,1,0:T(4,128)(2,1)} async-done(((bf16[1,4,2048]{2,1,0:T(4,128)(2,1)}), bf16[512,4,2048]{2,1,0:T(4,128)(2,1)}) %all-gather.7.cloned.1.call-update) | async-done | bytes 8388624 | tf_op jit(solution)/shard_map/all_gather | solution.py:82
  229.2 12.5 %reshape.304 = bf16[2048,2048]{1,0:T(8,128)(2,1)} reshape(bf16[512,4,2048]{2,1,0:T(4,128)(2,1)} %all-gather.7.cloned.1.call-done) | data formatting | bytes 16777216
  241.7 5.6 %fusion = f32[16,2048]{1,0:T(8,128)S(1)} fusion(bf16[16,2048]{0,1:T(8,128)(2,1)S(1)} %bitcast.111, bf16[2048,2048]{1,0:T(8,128)(2,1)} %reshape.304, f32[16]{0:T(128)S(1)} %convert_bitcast_fusion, f32[2048]{0:T(1024)S(1)} %bitcast.113), kind=kOutput, calls=%fused_computation.3 | convolution fusion | flops 134283264 | bytes 8593472 | tf_op jit(solution)/shard_map/dot_general | solution.py:104
  247.5 0.5 convolution_bitcast_fusion
  247.9 0.4 convolution_bitcast_fusion.1
  248.4 0.5 fusion.20
  248.9 0.5 fusion.19
  249.4 0.5 fusion.8
  250.4 0.5 fusion.7
  251.3 0.6 multiply_subtract_fusion.2
  252.0 1.0 copy.35
  253.0 3.6 reshape.328
  256.6 10.0 %all-to-all-start.1 = ((f32[128,1,512]{2,1,0:T(1,128)}), f32[128,1,512]{2,1,0:T(1,128)S(1)}, u32[]{:S(2)}, u32[]{:S(2)}) async-start(f32[128,1,512]{2,1,0:T(1,128)} %reshape.328), calls=%async_computation.1 | async-start | bytes 524288 | tf_op jit(solution)/shard_map/all_to_all | solution.py:116
  266.6 0.5 broadcast.267
  267.1 0.7 fusion.127
  268.1 13.7 %all-to-all-done.1 = f32[128,1,512]{2,1,0:T(1,128)S(1)} async-done(((f32[128,1,512]{2,1,0:T(1,128)}), f32[128,1,512]{2,1,0:T(1,128)S(1)}, u32[]{:S(2)}, u32[]{:S(2)}) %all-to-all-start.1) | async-done | bytes 262176 | tf_op jit(solution)/shard_map/all_to_all | solution.py:116
  281.8 0.5 broadcast.268
  282.3 1.2 reduce.9
  283.6 2.8 reshape.329
  286.4 2.6 copy.51
  288.9 3.2 copy.46
  292.2 3.6 reshape.330
  295.8 3.7 %all-to-all-start.2 = ((f32[4,1,16384]{2,1,0:T(1,128)}), f32[4,1,16384]{2,1,0:T(1,128)S(1)}, u32[]{:S(2)}, u32[]{:S(2)}) async-start(f32[4,1,16384]{2,1,0:T(1,128)} %reshape.330), calls=%async_computation.2 | async-start | bytes 524288 | tf_op jit(solution)/shard_map/all_to_all | solution.py:115
  299.5 5.8 %all-to-all-done.2 = f32[4,1,16384]{2,1,0:T(1,128)S(1)} async-done(((f32[4,1,16384]{2,1,0:T(1,128)}), f32[4,1,16384]{2,1,0:T(1,128)S(1)}, u32[]{:S(2)}, u32[]{:S(2)}) %all-to-all-start.2) | async-done | bytes 262176 | tf_op jit(solution)/shard_map/all_to_all | solution.py:115
  305.3 1.3 reduce.10
  306.6 2.8 reshape.331
  309.4 2.4 fusion.128
  311.9 1.6 copy.47
  315.6 0.5 fusion.22
  316.1 0.5 fusion.21
  316.6 0.5 fusion.6
  317.5 0.5 fusion.4
  318.4 0.6 gather_fusion
  319.1 9.5 %all_gather.15 = f32[128,256]{1,0:T(8,128)S(1)} all-gather(f32[32,256]{1,0:T(8,128)S(1)} %broadcast_select_fusion), channel_id=1, replica_groups=mesh['row'=128,'ex'=4] {'ex'}, dimensions={0}, use_global_device_ids=true | all-gather | bytes 163840 | tf_op jit(solution)/shard_map/all_gather | solution.py:130
  328.6 1.1 scatter_custom_fusion
  329.8 24.0 %all_to_all.51 = f32[128,2,256]{2,1,0:T(2,128)S(1)} all-to-all(f32[128,2,256]{2,1,0:T(2,128)S(1)} %all_to_all.45), channel_id=1, replica_groups=mesh['row'=128,'ex'=4] {'row'}, dimensions={0} | all-to-all | bytes 524288 | tf_op jit(solution)/shard_map/all_to_all | solution.py:136
  353.8 0.7 copy.54
  (36 shorter events, 5.7 us)
Async XLA Ops:
  6.5 92.9 %all-gather.5.cloned.1.call-start = ((), (), s32[]{:S(2)}) async-start(), calls=%async_computation.4 | async-start | bytes 2113536 | tf_op jit(solution)/shard_map/all_gather | solution.py:81
  7.3 222.0 %all-gather.7.cloned.1.call-start = ((), (), s32[]{:S(2)}) async-start(), calls=%async_computation.5 | async-start | bytes 8404992 | tf_op jit(solution)/shard_map/all_gather | solution.py:82
  103.3 20.9 %all-to-all-start = ((bf16[128,2,128]{2,1,0:T(2,128)(2,1)}), bf16[128,2,128]{2,1,0:T(2,128)(2,1)S(1)}, u32[]{:S(2)}, u32[]{:S(2)}) async-start(bf16[128,2,128]{2,1,0:T(2,128)(2,1)} %reshape.326), calls=%async_computation | async-start | bytes 131072 | tf_op jit(solution)/shard_map/all_to_all | solution.py:103
  251.9 15.2 %copy-start = (s32[1,1,4,32,1]{3,4,2,1,0:T(1,128)S(1)}, s32[1,1,4,32,1]{3,4,2,1,0:T(1,128)}, u32[]{:S(2)}) copy-start(s32[1,1,4,32,1]{3,4,2,1,0:T(1,128)} %param.13) | copy-start | bytes 1540
  256.6 25.2 %all-to-all-start.1 = ((f32[128,1,512]{2,1,0:T(1,128)}), f32[128,1,512]{2,1,0:T(1,128)S(1)}, u32[]{:S(2)}, u32[]{:S(2)}) async-start(f32[128,1,512]{2,1,0:T(1,128)} %reshape.328), calls=%async_computation.1 | async-start | bytes 524288 | tf_op jit(solution)/shard_map/all_to_all | solution.py:116
  292.2 7.3 %copy-start.1 = (s32[1,1,1,32]{3,2,1,0:T(1,128)S(1)}, s32[1,1,1,32]{3,2,1,0:T(1,128)}, u32[]{:S(2)}) copy-start(s32[1,1,1,32]{3,2,1,0:T(1,128)} %param.12) | copy-start | bytes 388
  295.8 9.5 %all-to-all-start.2 = ((f32[4,1,16384]{2,1,0:T(1,128)}), f32[4,1,16384]{2,1,0:T(1,128)S(1)}, u32[]{:S(2)}, u32[]{:S(2)}) async-start(f32[4,1,16384]{2,1,0:T(1,128)} %reshape.330), calls=%async_computation.2 | async-start | bytes 524288 | tf_op jit(solution)/shard_map/all_to_all | solution.py:115
Sparse Core Ops, SparseCore 0:
  10.5 88.9 all-gather.4
  103.9 125.2 all-gather.6
where the time goes:
time: 362 us; the launch traced here: 361 us
  waiting for transfers between devices  215 us (59%)
  blocking collectives  44.2 us (12%)
  local copies, waits for them, and re-layouts  44.1 us (12%)
  starting transfers between devices  23.1 us (6%)
  matrix products  14.3 us (4%)
  between operations  13.8 us (4%)
  other arithmetic  6.33 us (2%)
    all_gather x1, waiting for transfers between devices, shards(): left_full = lax.all_gather(left_inv, ('row', 'ex'), axis=0, tiled=True)  105 us
    all_gather x1, waiting for transfers between devices, shards(): right_cols = lax.all_gather(right_inv, 'row', axis=0, tiled=True)  79.2 us
    unnamed x13, local copies, waits for them, and re-layouts  27.9 us
    all_to_all x1, blocking collectives, shards(): lax.all_to_all(outgoing, 'row', split_axis=0, concat_axis=0, tiled=True)  24 us
    all_to_all x1, waiting for transfers between devices, shards(): lax.all_to_all(stacked, 'row', split_axis=2, concat_axis=1, tiled=True)  13.7 us
    all_gather x1, blocking collectives, shards(): rows_all = lax.all_gather(own_rows, 'ex', axis=0, tiled=True)  10.7 us
    all_to_all x1, waiting for transfers between devices, shards(): lax.all_to_all(projected, 'row', split_axis=0, concat_axis=1, tiled=True)  10.6 us
    all_to_all x1, starting transfers between devices, shards(): lax.all_to_all(stacked, 'row', split_axis=2, concat_axis=1, tiled=True)  9.99 us
  transfers between devices with their start and end apart: 5, of which 5 were waited for; matrix products, arithmetic and copies ran while one was open for 2% of the time, Pallas kernels for 0%

commit v1 on v0

--- a/solution.py
+++ b/solution.py
@@ -79,7 +79,12 @@
     block_count = local_rows * (width // BLOCK)
     capacity = max(2, 2 * ex_count * list_len // row_count)
     right_cols = lax.all_gather(right_inv, "row", axis=0, tiled=True)
-    left_full = lax.all_gather(left_inv, ("row", "ex"), axis=0, tiled=True)
+    left_full = jnp.concatenate(
+        lax.all_to_all(
+            jnp.stack([left_inv for _ in range(lax.axis_size(("row", "ex")))]), ("row", "ex"), 0, 0
+        ),
+        axis=0,
+    )
     pair_start = row_id * local_rows
     my_example = pair_start // ex_cols
     col_start = ex_id * ex_cols + pair_start % ex_cols

time: 362 us -> 469 us (1.30); the launches traced: 361 us -> 462 us
  waiting for transfers between devices: 215 us -> 286 us
  blocking collectives: 44.2 us -> 65 us
  local copies, waits for them, and re-layouts: 44.1 us -> 51.1 us
    all_to_all x1, waiting for transfers between devices: 10.6 us -> 184 us  [shards(): lax.all_to_all(jnp.stack([left_inv for _ in range(lax.axis_size(('row', '...]
    all_gather x1 -> x0, waiting for transfers between devices: 105 us -> none  [shards(): left_full = lax.all_gather(left_inv, ('row', 'ex'), axis=0, tiled=True)]
    all_to_all x0 -> x1, blocking collectives: none -> 20.8 us  [shards(): lax.all_to_all(projected, 'row', split_axis=0, concat_axis=1, tiled=True)]
    unnamed x13 -> x14, local copies, waits for them, and re-layouts: 27.9 us -> 14.8 us
    reshape x0 -> x1, local copies, waits for them, and re-layouts: none -> 12.5 us  [shards(): jnp.concatenate(lax.all_to_all(jnp.stack([left_inv for _ in range(lax.axi...]
    another operation x0 -> x1, local copies, waits for them, and re-layouts: none -> 7.49 us  [shards(): jnp.stack([left_inv for _ in range(lax.axis_size(('row', 'ex')))])]
  transfers between devices with their start and end apart: 5 -> 4, of which waited for: 5 -> 4; matrix products, arithmetic and copies ran while one was open for 2% -> 1% of each run, Pallas kernels for 0% -> 0%
where the time goes in v1:
time: 469 us; the launch traced here: 462 us
  waiting for transfers between devices  286 us (61%)
  blocking collectives  65 us (14%)
  local copies, waits for them, and re-layouts  51.1 us (11%)
  starting transfers between devices  26.5 us (6%)
  matrix products  14.3 us (3%)
  between operations  14 us (3%)
  other arithmetic  5.74 us (1%)
    all_to_all x1, waiting for transfers between devices, shards(): lax.all_to_all(jnp.stack([left_inv for _ in range(lax.axis_size(('row', '...  184 us
    all_gather x1, waiting for transfers between devices, shards(): right_cols = lax.all_gather(right_inv, 'row', axis=0, tiled=True)  81.5 us
    all_to_all x1, blocking collectives, shards(): lax.all_to_all(outgoing, 'row', split_axis=0, concat_axis=0, tiled=True)  24 us
    all_to_all x1, blocking collectives, shards(): lax.all_to_all(projected, 'row', split_axis=0, concat_axis=1, tiled=True)  20.8 us
    unnamed x14, local copies, waits for them, and re-layouts  14.8 us
    all_to_all x1, waiting for transfers between devices, shards(): lax.all_to_all(stacked, 'row', split_axis=2, concat_axis=1, tiled=True)  13.5 us
    reshape x1, local copies, waits for them, and re-layouts, shards(): jnp.concatenate(lax.all_to_all(jnp.stack([left_inv for _ in range(lax.axi...  12.5 us
    all_to_all x1, starting transfers between devices, shards(): lax.all_to_all(jnp.stack([left_inv for _ in range(lax.axis_size(('row', '...  12.3 us
  transfers between devices with their start and end apart: 4, of which 4 were waited for; matrix products, arithmetic and copies ran while one was open for 1% of the time, Pallas kernels for 0%

profile of v1, /device:TPU:1, one launch (start us, length us, event | category | flops | bytes accessed | tf_op | source)
XLA Modules:
  0.0 462.2 jit_solution(3392728466933052697)
XLA Ops:
  6.5 0.7 all-gather.3.cloned.1.call-update
  7.3 10.7 %all-gather = bf16[4,1,16,2048]{3,2,1,0:T(8,128)(2,1)S(1)} all-gather(bf16[1,1,16,2048]{3,2,1,0:T(8,128)(2,1)} %param.7), channel_id=2, replica_groups=mesh['row'=128,'ex'=4] {'ex'}, dimensions={0}, use_global_device_ids=true | all-gather | bytes 327680 | tf_op jit(solution)/shard_map/all_gather | solution.py:103
  18.0 81.5 %all-gather.3.cloned.1.call-done = bf16[2048,512]{1,0:T(8,128)(2,1)} async-done(((bf16[16,512]{1,0:T(8,128)(2,1)}), bf16[2048,512]{1,0:T(8,128)(2,1)}) %all-gather.3.cloned.1.call-update) | async-done | bytes 2097168 | tf_op jit(solution)/shard_map/all_gather | solution.py:81
  99.5 2.1 fusion.12
  102.7 20.8 %all_to_all.56 = bf16[128,2,128]{2,1,0:T(2,128)(2,1)S(1)} all-to-all(bf16[128,2,128]{2,1,0:T(2,128)(2,1)S(1)} %reshape.330), channel_id=1, replica_groups=mesh['row'=128,'ex'=4] {'row'}, dimensions={0} | all-to-all | bytes 131072 | tf_op jit(solution)/shard_map/all_to_all | solution.py:108
  123.5 7.5 %stack.4 = bf16[512,4,2048]{2,1,0:T(4,128)(2,1)} broadcast(bf16[4,2048]{1,0:T(4,128)(2,1)S(1)} %copy-done), dimensions={1,2} | broadcast | bytes 8404992 | tf_op jit(solution)/shard_map/stack | solution.py:84
  131.0 12.3 %all-to-all-start.1 = ((bf16[512,4,2048]{2,1,0:T(4,128)(2,1)}), bf16[512,4,2048]{2,1,0:T(4,128)(2,1)}, u32[]{:S(2)}, u32[]{:S(2)}) async-start(bf16[512,4,2048]{2,1,0:T(4,128)(2,1)} %stack.4), calls=%async_computation.1 | async-start | bytes 16777216 | tf_op jit(solution)/shard_map/all_to_all | solution.py:83
  143.3 0.8 convert_bitcast_fusion
  144.2 0.8 subtract_convert_fusion
  145.3 183.8 %all-to-all-done.1 = bf16[512,4,2048]{2,1,0:T(4,128)(2,1)} async-done(((bf16[512,4,2048]{2,1,0:T(4,128)(2,1)}), bf16[512,4,2048]{2,1,0:T(4,128)(2,1)}, u32[]{:S(2)}, u32[]{:S(2)}) %all-to-all-start.1) | async-done | bytes 8388640 | tf_op jit(solution)/shard_map/all_to_all | solution.py:83
  329.1 12.5 %reshape.288 = bf16[2048,2048]{1,0:T(8,128)(2,1)} reshape(bf16[512,4,2048]{2,1,0:T(4,128)(2,1)} %all-to-all-done.1) | data formatting | bytes 16777216 | tf_op jit(solution)/shard_map/reshape | solution.py:82
  341.6 5.6 %fusion = f32[16,2048]{1,0:T(8,128)S(1)} fusion(bf16[16,2048]{0,1:T(8,128)(2,1)S(1)} %bitcast.110, bf16[2048,2048]{1,0:T(8,128)(2,1)} %reshape.288, f32[16]{0:T(128)S(1)} %convert_bitcast_fusion, f32[2048]{0:T(1024)S(1)} %bitcast.112), kind=kOutput, calls=%fused_computation.3 | convolution fusion | flops 134283264 | bytes 8593472 | tf_op jit(solution)/shard_map/dot_general | solution.py:109
  347.4 0.5 convolution_bitcast_fusion
  347.8 0.4 convolution_bitcast_fusion.1
  348.3 0.5 fusion.20
  348.8 0.5 fusion.19
  349.3 0.5 fusion.8
  350.3 0.5 fusion.7
  351.2 0.6 multiply_subtract_fusion.2
  351.9 1.0 copy.35
  352.9 3.6 reshape.332
  356.5 10.6 %all-to-all-start.2 = ((f32[128,1,512]{2,1,0:T(1,128)}), f32[128,1,512]{2,1,0:T(1,128)S(1)}, u32[]{:S(2)}, u32[]{:S(2)}) async-start(f32[128,1,512]{2,1,0:T(1,128)} %reshape.332), calls=%async_computation.2 | async-start | bytes 524288 | tf_op jit(solution)/shard_map/all_to_all | solution.py:121
  367.1 0.6 broadcast.269
  367.7 0.7 fusion.127
  368.7 13.5 %all-to-all-done.2 = f32[128,1,512]{2,1,0:T(1,128)S(1)} async-done(((f32[128,1,512]{2,1,0:T(1,128)}), f32[128,1,512]{2,1,0:T(1,128)S(1)}, u32[]{:S(2)}, u32[]{:S(2)}) %all-to-all-start.2) | async-done | bytes 262176 | tf_op jit(solution)/shard_map/all_to_all | solution.py:121
  382.2 0.5 broadcast.270
  382.8 1.2 reduce.9
  384.0 2.8 reshape.333
  386.8 2.6 copy.51
  389.4 3.2 copy.46
  392.6 3.6 reshape.334
  396.2 3.6 all-to-all-start.3
  399.9 6.0 %all-to-all-done.3 = f32[4,1,16384]{2,1,0:T(1,128)S(1)} async-done(((f32[4,1,16384]{2,1,0:T(1,128)}), f32[4,1,16384]{2,1,0:T(1,128)S(1)}, u32[]{:S(2)}, u32[]{:S(2)}) %all-to-all-start.3) | async-done | bytes 262176 | tf_op jit(solution)/shard_map/all_to_all | solution.py:120
  405.9 1.3 reduce.10
  407.2 2.8 reshape.335
  410.0 2.5 fusion.128
  412.5 1.6 copy.47
  414.5 0.4 fusion.41
  415.4 0.4 convolution_subtract_fusion.1
  416.3 0.5 fusion.22
  416.8 0.5 fusion.21
  417.3 0.5 fusion.6
  418.2 0.5 fusion.4
  419.1 0.6 gather_fusion
  419.8 9.5 %all_gather.11 = f32[128,256]{1,0:T(8,128)S(1)} all-gather(f32[32,256]{1,0:T(8,128)S(1)} %broadcast_select_fusion), channel_id=1, replica_groups=mesh['row'=128,'ex'=4] {'ex'}, dimensions={0}, use_global_device_ids=true | all-gather | bytes 163840 | tf_op jit(solution)/shard_map/all_gather | solution.py:135
  429.3 1.1 scatter_custom_fusion
  430.5 24.0 %all_to_all.57 = f32[128,2,256]{2,1,0:T(2,128)S(1)} all-to-all(f32[128,2,256]{2,1,0:T(2,128)S(1)} %all_to_all.49), channel_id=1, replica_groups=mesh['row'=128,'ex'=4] {'row'}, dimensions={0} | all-to-all | bytes 524288 | tf_op jit(solution)/shard_map/all_to_all | solution.py:141
  454.4 0.7 copy.54
  (37 shorter events, 5.1 us)
Async XLA Ops:
  6.5 92.9 %all-gather.3.cloned.1.call-start = ((), (), s32[]{:S(2)}) async-start(), calls=%async_computation.5 | async-start | bytes 2113536 | tf_op jit(solution)/shard_map/all_gather | solution.py:81
  101.5 21.9 %copy-start = (bf16[4,2048]{1,0:T(4,128)(2,1)S(1)}, bf16[4,2048]{1,0:T(4,128)(2,1)}, u32[]{:S(2)}) copy-start(bf16[4,2048]{1,0:T(4,128)(2,1)} %param.9) | copy-start | bytes 49156
  131.0 13.2 %copy-start.2 = (s32[1,1,1,32]{3,2,1,0:T(1,128)S(1)}, s32[1,1,1,32]{3,2,1,0:T(1,128)}, u32[]{:S(2)}) copy-start(s32[1,1,1,32]{3,2,1,0:T(1,128)} %param.12) | copy-start | bytes 388
  131.0 198.2 %all-to-all-start.1 = ((bf16[512,4,2048]{2,1,0:T(4,128)(2,1)}), bf16[512,4,2048]{2,1,0:T(4,128)(2,1)}, u32[]{:S(2)}, u32[]{:S(2)}) async-start(bf16[512,4,2048]{2,1,0:T(4,128)(2,1)} %stack.4), calls=%async_computation.1 | async-start | bytes 16777216 | tf_op jit(solution)/shard_map/all_to_all | solution.py:83
  351.8 15.9 %copy-start.1 = (s32[1,1,4,32,1]{3,4,2,1,0:T(1,128)S(1)}, s32[1,1,4,32,1]{3,4,2,1,0:T(1,128)}, u32[]{:S(2)}) copy-start(s32[1,1,4,32,1]{3,4,2,1,0:T(1,128)} %param.13) | copy-start | bytes 1540
  356.5 25.7 %all-to-all-start.2 = ((f32[128,1,512]{2,1,0:T(1,128)}), f32[128,1,512]{2,1,0:T(1,128)S(1)}, u32[]{:S(2)}, u32[]{:S(2)}) async-start(f32[128,1,512]{2,1,0:T(1,128)} %reshape.332), calls=%async_computation.2 | async-start | bytes 524288 | tf_op jit(solution)/shard_map/all_to_all | solution.py:121
  396.2 9.7 %all-to-all-start.3 = ((f32[4,1,16384]{2,1,0:T(1,128)}), f32[4,1,16384]{2,1,0:T(1,128)S(1)}, u32[]{:S(2)}, u32[]{:S(2)}) async-start(f32[4,1,16384]{2,1,0:T(1,128)} %reshape.334), calls=%async_computation.3 | async-start | bytes 524288 | tf_op jit(solution)/shard_map/all_to_all | solution.py:120
Sparse Core Ops, SparseCore 0:
  10.5 88.9 all-gather.2
